TPU v7x, 32 devices: a whole 2x2x4 slice. The times are simulated.
32 devices in a mesh: groups: 2 (over x), gy: 16 (over z, y, core).
Axes of the slice: x: 2, y: 2, z: 4, core: 2. Of those that a mesh axis runs over, the one named last changes fastest.
Arguments:
- observed: float32 [2048, 16, 256], P(('groups', 'gy')), parts along dimension 0, may hold values from -6 to 6
- tf_table: float32 [16], replicated, may hold values from 0.2 to 2
- tilt_index: int32 [513, 129], replicated, may hold values from 0 to 15
- wedge: int32 [513, 129], replicated, may hold values 0 or 1
Outputs:
- restored: float32 [2048, 16, 256], P(('groups', 'gy')), parts along dimension 0
There are 2 independent parts, one for each index of `groups`. A program takes and returns all parts, laid end to end along the dimension named above; an argument that names none is the same for every part. Nothing has to cross between parts.
All inputs are finite; a program needn't handle non-finite values.
Results may differ from a plain program's by a relative error of at most 0.00011.
Values sent between devices are 32-bit elements; how exact they have to be, the bound alone decides.
A program may use at most 64 MiB of HBM per device.

v0:
```python
import math
import jax
import jax.numpy as jnp
from jax import lax
from jax.sharding import PartitionSpec as P

NX = 1024
OUTER = 2
PASSES = 2
step_dual = 0.14
step_primal = 0.14
huber_eps = 0.05
bound_dual = 0.5
highest = lax.Precision.HIGHEST


def extended(value, sides, width):
    for axis, dim in sides:
        devices, length = (lax.axis_size(axis), value.shape[dim])
        up = [(i, (i + 1) % devices) for i in range(devices - 1)]
        down = [(j, i) for i, j in up]
        last = lax.slice_in_dim(value, length - width, length, axis=dim)
        initial = lax.slice_in_dim(value, 0, width, axis=dim)
        before = lax.ppermute(last, axis, up)
        after = lax.ppermute(initial, axis, down)
        value = jnp.concatenate([before, value, after], axis=dim)
    return value


def curvature(field, axis):
    widths = [(0, 0), (0, 0), (0, 0)]
    widths[axis] = (1, 1)
    padded = jnp.pad(field, widths)
    upper = lax.slice_in_dim(padded, 2, padded.shape[axis], axis=axis)
    lower = lax.slice_in_dim(padded, 0, padded.shape[axis] - 2, axis=axis)
    return upper + lower - 2.0 * field


def rim_curvature(padded, field, axis):
    upper = lax.slice_in_dim(padded, 2, padded.shape[axis], axis=axis)
    lower = lax.slice_in_dim(padded, 0, padded.shape[axis] - 2, axis=axis)
    return upper + lower - 2.0 * field


def denoise(target, duals, sharded, primal_rim, dual_rim):
    field = target
    lead = target
    for sweep in range(PASSES):
        padded = primal_rim(lead)
        raised = []
        for axis in range(3):
            if axis == sharded:
                bend = rim_curvature(padded, lead, axis)
            else:
                bend = curvature(lead, axis)
            raised.append(
                (duals[axis] + step_dual * bend) / (1.0 + step_dual * huber_eps / bound_dual)
            )
        total = raised[0] * raised[0] + raised[1] * raised[1] + raised[2] * raised[2]
        shrink = jnp.sqrt(jnp.maximum(1.0, total / (bound_dual * bound_dual)))
        duals = (raised[0] / shrink, raised[1] / shrink, raised[2] / shrink)
        padded_dual = dual_rim(duals[sharded])
        adjoint = jnp.zeros_like(field)
        for axis in range(3):
            if axis == sharded:
                adjoint = rim_curvature(padded_dual, duals[axis], axis)
            else:
                adjoint = adjoint + curvature(duals[axis], axis)
        updated = (field - step_primal * adjoint + step_primal * target) / (1.0 + step_primal)
        lead = 2.0 * updated - field
        field = updated
    return (field, duals)


def z_tables(length):
    half = length // 2
    position = jnp.arange(length, dtype=jnp.int32)
    column = jnp.arange(length, dtype=jnp.int32)
    is_cosine = column <= half
    frequency = jnp.where(is_cosine, column, column - half)
    phase = position[:, None] * frequency[None, :] % length
    angle = phase.astype(jnp.float32) * (2.0 * math.pi / length)
    forward = jnp.where(is_cosine[None, :], jnp.cos(angle), jnp.sin(angle))
    weight = jnp.where((column == 0) | (column == half), 1.0, 2.0) / length
    backward = forward.T * weight[:, None]
    return (forward, backward)


def x_tables(length):
    half = length // 2
    freqs = jnp.arange(half + 1, dtype=jnp.int32)
    position = jnp.arange(length, dtype=jnp.int32)
    phase = freqs[:, None] * position[None, :] % length
    angle = phase.astype(jnp.float32) * (2.0 * math.pi / length)
    cos_table = jnp.cos(angle)
    sin_table = jnp.sin(angle)
    weight = jnp.where((freqs == 0) | (freqs == half), 1.0, 2.0) / length
    return (cos_table, sin_table, (cos_table * weight[:, None]).T, (sin_table * weight[:, None]).T)


def x_forward(columns, cos_table, sin_table):
    flat = columns.reshape(columns.shape[0], -1)
    shape_out = (cos_table.shape[0],) + columns.shape[1:]
    real_part = jnp.dot(cos_table, flat, precision=highest).reshape(shape_out)
    imag_part = jnp.dot(sin_table, flat, precision=highest).reshape(shape_out)
    return (real_part, imag_part)


def x_inverse(real_part, imag_part, cos_back, sin_back):
    rows = real_part.shape[0]
    flat_real = real_part.reshape(rows, -1)
    flat_imag = imag_part.reshape(rows, -1)
    summed = jnp.dot(cos_back, flat_real, precision=highest) + jnp.dot(
        sin_back, flat_imag, precision=highest
    )
    return summed.reshape((cos_back.shape[0],) + real_part.shape[1:])


def filters(tf_table, tilt_index, wedge, length_z):
    levels = jnp.arange(tf_table.shape[0], dtype=jnp.int32)
    picked = jnp.sum(jnp.where(tilt_index[:, :, None] == levels, tf_table, 0.0), axis=2)
    half_rows = picked * wedge.astype(jnp.float32)
    response = jnp.concatenate([half_rows, half_rows[:, 1 : length_z // 2]], 1)
    denom = response * response + 1.0
    return ((response / denom)[:, None, :], (1.0 / denom)[:, None, :])


def rim_x_primal(field):
    return extended(field, (("gy", 0),), 1)


def rim_x_dual(field):
    return extended(field, (("gy", 0),), 1)


def local(observed, tf_table, tilt_index, wedge):
    length_z = observed.shape[2]
    forward_z, backward_z = z_tables(length_z)
    cos_table, sin_table, cos_back, sin_back = x_tables(NX)
    g_data, g_prior = filters(tf_table, tilt_index, wedge, length_z)
    packed = jnp.dot(observed, forward_z, precision=highest)
    columns = lax.all_to_all(packed, "gy", split_axis=1, concat_axis=0, tiled=True)
    data_real, data_imag = x_forward(columns, cos_table, sin_table)
    prior_real, prior_imag = (data_real, data_imag)
    current = observed
    duals = (jnp.zeros_like(observed), jnp.zeros_like(observed), jnp.zeros_like(observed))
    for outer in range(OUTER):
        if outer > 0:
            again = lax.all_to_all(
                jnp.dot(current, forward_z, precision=highest),
                "gy",
                split_axis=1,
                concat_axis=0,
                tiled=True,
            )
            prior_real, prior_imag = x_forward(again, cos_table, sin_table)
        merged = x_inverse(
            g_data * data_real + g_prior * prior_real,
            g_data * data_imag + g_prior * prior_imag,
            cos_back,
            sin_back,
        )
        slabs = lax.all_to_all(merged, "gy", split_axis=0, concat_axis=1, tiled=True)
        target = jnp.dot(slabs, backward_z, precision=highest)
        current, duals = denoise(target, duals, 0, rim_x_primal, rim_x_dual)
    return current


def solution(mesh):
    in_specs = (P(("groups", "gy"), None, None), P(), P(), P())
    out_specs = P(("groups", "gy"), None, None)
    return jax.shard_map(local, mesh=mesh, in_specs=in_specs, out_specs=out_specs, check_vma=False)
```

profile of v0, /device:TPU:8, one launch (start us, length us, event | category | flops | bytes accessed | tf_op | source)
XLA Modules:
  0.0 304.0 jit_solution(17991332169227890438)
XLA Ops:
  1.2 3.4 %convolution_bitcast_fusion = f32[64,16,256]{2,0,1:T(8,128)} fusion(f32[64,16,256]{2,1,0:T(8,128)S(1)} %copy-done, s32[256]{0:T(256)S(1)} %add_select_fusion.3, pred[256]{0:T(512)(128)(4,1)S(1)} %iota_compare_fusion.3), kind=kOutput, calls=%fused_computation.55 | convolution fusion | flops 806289408 | bytes 2098432 | tf_op jit(solution)/shard_map/dot_general | solution.py:141
  4.7 6.9 %all-to-all-start = ((f32[64,16,256]{2,0,1:T(8,128)}), f32[64,16,256]{2,0,1:T(8,128)S(1)}, u32[]{:S(2)}, u32[]{:S(2)}) async-start(f32[64,16,256]{2,0,1:T(8,128)} %convolution_bitcast_fusion), calls=%async_computation | async-start | bytes 2097152 | tf_op jit(solution)/shard_map/all_to_all | solution.py:142
  11.6 1.8 select_reduce_fusion
  13.5 21.7 %all-to-all-done = f32[64,16,256]{2,0,1:T(8,128)S(1)} async-done(((f32[64,16,256]{2,0,1:T(8,128)}), f32[64,16,256]{2,0,1:T(8,128)S(1)}, u32[]{:S(2)}, u32[]{:S(2)}) %all-to-all-start) | async-done | bytes 1048608 | tf_op jit(solution)/shard_map/all_to_all | solution.py:142
  35.2 10.8 %fusion.41 = f32[513,256]{0,1:T(8,128)S(1)} fusion(f32[1024,256]{1,0:T(8,128)S(1)} %bitcast.46), kind=kOutput, calls=%fused_computation.67 | convolution fusion | flops 1621112832 | bytes 1573888 | tf_op jit(solution)/shard_map/dot_general | solution.py:105
  46.0 10.5 %fusion.36 = f32[513,256]{0,1:T(8,128)S(1)} fusion(f32[1024,256]{1,0:T(8,128)S(1)} %bitcast.47), kind=kOutput, calls=%fused_computation.66 | convolution fusion | flops 1621112832 | bytes 1573888 | tf_op jit(solution)/shard_map/dot_general | solution.py:104
  56.5 12.6 %fusion.8 = f32[1024,256]{1,0:T(8,128)S(1)} fusion(f32[513]{0:T(1024)S(1)} %select_multiply_fusion.3, f32[513,256]{0,1:T(8,128)S(1)} %fusion.41, f32[513,127]{0,1:T(8,128)S(1)} %slice.276, f32[513,129]{0,1:T(8,128)S(1)} %convert_multiply_fusion), kind=kOutput, calls=%fused_computation.13 | convolution fusion | flops 1622688768 | bytes 2101252 | tf_op jit(solution)/shard_map/dot_general | solution.py:113
  69.1 12.1 %fusion.17 = f32[1024,1,256]{2,0,1:T(8,128)S(1)} fusion(f32[1024,256]{1,0:T(8,128)S(1)} %fusion.8, f32[513]{0:T(1024)S(1)} %select_multiply_fusion.3, f32[513,256]{0,1:T(8,128)S(1)} %fusion.36, f32[513,127]{0,1:T(8,128)S(1)} %slice.276, f32[513,129]{0,1:T(8,128)S(1)} %convert_multiply_fusion), kind=kOutput, calls=%fused_computation.52 | convolution fusion | flops 1622950912 | bytes 3149828 | tf_op jit(solution)/shard_map/dot_general | solution.py:113
  81.2 2.0 copy.43
  83.3 5.6 %all-to-all-start.1 = ((f32[1024,1,256]{2,1,0:T(1,128)}), f32[1024,1,256]{2,1,0:T(1,128)S(1)}, u32[]{:S(2)}, u32[]{:S(2)}) async-start(f32[1024,1,256]{2,1,0:T(1,128)} %copy.43), calls=%async_computation.1 | async-start | bytes 2097152 | tf_op jit(solution)/shard_map/all_to_all | solution.py:163
  88.9 24.1 %all-to-all-done.1 = f32[1024,1,256]{2,1,0:T(1,128)S(1)} async-done(((f32[1024,1,256]{2,1,0:T(1,128)}), f32[1024,1,256]{2,1,0:T(1,128)S(1)}, u32[]{:S(2)}, u32[]{:S(2)}) %all-to-all-start.1) | async-done | bytes 1048608 | tf_op jit(solution)/shard_map/all_to_all | solution.py:163
  113.0 2.6 fusion.146
  115.7 2.5 collective-permute-start
  118.2 2.3 collective-permute-start.1
  120.5 3.7 %collective-permute-done.1 = f32[1,16,256]{2,1,0:T(8,128)S(1)} collective-permute-done((f32[1,16,256]{2,1,0:T(8,128)S(1)}, f32[1,16,256]{2,1,0:T(8,128)S(1)}, u32[]{:S(2)}, u32[]{:S(2)}) %collective-permute-start.1) | collective-permute-done | bytes 16416 | tf_op jit(solution)/shard_map/ppermute | solution.py:24
  125.5 1.9 collective-permute-start.2
  127.4 2.4 collective-permute-start.3
  130.6 2.7 collective-permute-done.3
  134.3 1.9 collective-permute-start.4
  136.3 2.4 collective-permute-start.5
  138.7 3.5 %collective-permute-done.5 = f32[1,16,256]{2,1,0:T(8,128)S(1)} collective-permute-done((f32[1,16,256]{2,1,0:T(8,128)S(1)}, f32[1,16,256]{2,1,0:T(8,128)S(1)}, u32[]{:S(2)}, u32[]{:S(2)}) %collective-permute-start.5) | collective-permute-done | bytes 16416 | tf_op jit(solution)/shard_map/ppermute | solution.py:24
  142.2 1.6 fusion.238
  143.8 1.9 collective-permute-start.6
  145.7 2.4 collective-permute-start.7
  148.6 3.1 %collective-permute-done.7 = f32[1,16,256]{2,1,0:T(8,128)S(1)} collective-permute-done((f32[1,16,256]{2,1,0:T(8,128)S(1)}, f32[1,16,256]{2,1,0:T(8,128)S(1)}, u32[]{:S(2)}, u32[]{:S(2)}) %collective-permute-start.7) | collective-permute-done | bytes 16416 | tf_op jit(solution)/shard_map/ppermute | solution.py:24
  152.7 2.5 fusion.148
  155.3 30.2 %all_to_all.66 = f32[64,16,256]{2,0,1:T(8,128)S(1)} all-to-all(f32[64,16,256]{2,0,1:T(8,128)S(1)} %fusion.148), channel_id=1, replica_groups=mesh['groups'=2,'gy'=16] {'gy'}, dimensions={1} | all-to-all | bytes 2097152 | tf_op jit(solution)/shard_map/all_to_all | solution.py:149
  185.5 10.6 %fusion.26 = f32[513,256]{0,1:T(8,128)S(1)} fusion(f32[1024,256]{1,0:T(8,128)S(1)} %bitcast.48, f32[513,256]{0,1:T(8,128)S(1)} %copy-done.5, f32[513,127]{0,1:T(8,128)S(1)} %slice.276, f32[513,129]{0,1:T(8,128)S(1)} %convert_multiply_fusion), kind=kOutput, calls=%fused_computation.57 | convolution fusion | flops 1622163456 | bytes 2624512 | tf_op jit(solution)/shard_map/dot_general | solution.py:105
  196.1 10.8 %fusion.27 = f32[513,256]{0,1:T(8,128)S(1)} fusion(f32[1024,256]{1,0:T(8,128)S(1)} %bitcast.49, f32[513,256]{0,1:T(8,128)S(1)} %fusion.36, f32[513,127]{0,1:T(8,128)S(1)} %slice.276, f32[513,129]{0,1:T(8,128)S(1)} %convert_multiply_fusion), kind=kOutput, calls=%fused_computation.59 | convolution fusion | flops 1622163456 | bytes 2624512 | tf_op jit(solution)/shard_map/dot_general | solution.py:104
  206.9 12.1 %fusion.6 = f32[1024,256]{1,0:T(8,128)S(1)} fusion(f32[513,256]{0,1:T(8,128)S(1)} %fusion.26, f32[513]{0:T(1024)S(1)} %select_multiply_fusion.3), kind=kOutput, calls=%fused_computation.11 | convolution fusion | flops 1621638144 | bytes 1575940 | tf_op jit(solution)/shard_map/dot_general | solution.py:113
  219.1 12.3 %fusion.23 = f32[1024,1,256]{2,0,1:T(8,128)S(1)} fusion(f32[1024,256]{1,0:T(8,128)S(1)} %fusion.6, f32[513,256]{0,1:T(8,128)S(1)} %fusion.27, f32[513]{0:T(1024)S(1)} %select_multiply_fusion.3), kind=kOutput, calls=%fused_computation.54 | convolution fusion | flops 1621900288 | bytes 2624516 | tf_op jit(solution)/shard_map/dot_general | solution.py:113
  232.6 29.5 %all_to_all.67 = f32[1024,1,256]{2,1,0:T(1,128)S(1)} all-to-all(f32[1024,1,256]{2,1,0:T(1,128)S(1)} %copy.48), channel_id=1, replica_groups=mesh['groups'=2,'gy'=16] {'gy'}, dimensions={0} | all-to-all | bytes 2097152 | tf_op jit(solution)/shard_map/all_to_all | solution.py:163
  262.2 2.6 fusion.144
  264.8 3.2 %collective-permute-start.8 = (f32[1,16,256]{2,1,0:T(8,128)S(1)}, f32[1,16,256]{2,1,0:T(8,128)S(1)}, u32[]{:S(2)}, u32[]{:S(2)}) collective-permute-start(f32[1,16,256]{2,1,0:T(8,128)S(1)} %get-tuple-element.35), channel_id=1, source_target_pairs={{1,0},{2,1},{3,2},{4,3},{5,4},{6,5},{7,6},{8,7},{9,8},{10,9},{11,1... | collective-permute-start | bytes 49160 | tf_op jit(solution)/shard_map/ppermute | solution.py:25
  268.1 1.9 collective-permute-start.9
  270.0 4.0 %collective-permute-done.9 = f32[1,16,256]{2,1,0:T(8,128)S(1)} collective-permute-done((f32[1,16,256]{2,1,0:T(8,128)S(1)}, f32[1,16,256]{2,1,0:T(8,128)S(1)}, u32[]{:S(2)}, u32[]{:S(2)}) %collective-permute-start.9) | collective-permute-done | bytes 16416 | tf_op jit(solution)/shard_map/ppermute | solution.py:24
  274.1 1.6 fusion.239
  275.6 1.9 collective-permute-start.10
  277.6 2.4 collective-permute-start.11
  280.4 3.1 %collective-permute-done.11 = f32[1,16,256]{2,1,0:T(8,128)S(1)} collective-permute-done((f32[1,16,256]{2,1,0:T(8,128)S(1)}, f32[1,16,256]{2,1,0:T(8,128)S(1)}, u32[]{:S(2)}, u32[]{:S(2)}) %collective-permute-start.11) | collective-permute-done | bytes 16416 | tf_op jit(solution)/shard_map/ppermute | solution.py:24
  284.5 1.9 collective-permute-start.12
  286.4 2.4 collective-permute-start.13
  288.8 3.5 %collective-permute-done.13 = f32[1,16,256]{2,1,0:T(8,128)S(1)} collective-permute-done((f32[1,16,256]{2,1,0:T(8,128)S(1)}, f32[1,16,256]{2,1,0:T(8,128)S(1)}, u32[]{:S(2)}, u32[]{:S(2)}) %collective-permute-start.13) | collective-permute-done | bytes 16416 | tf_op jit(solution)/shard_map/ppermute | solution.py:24
  292.4 1.6 fusion.240
  293.9 1.9 collective-permute-start.14
  295.9 2.4 collective-permute-start.15
  298.7 3.1 %collective-permute-done.15 = f32[1,16,256]{2,1,0:T(8,128)S(1)} collective-permute-done((f32[1,16,256]{2,1,0:T(8,128)S(1)}, f32[1,16,256]{2,1,0:T(8,128)S(1)}, u32[]{:S(2)}, u32[]{:S(2)}) %collective-permute-start.15) | collective-permute-done | bytes 16416 | tf_op jit(solution)/shard_map/ppermute | solution.py:24
  301.8 2.0 fusion.115
  (45 shorter events, 9.1 us)
Async XLA Ops:
  0.0 1.2 copy-start
  4.7 6.9 %copy-start.1 = (s32[513,129]{0,1:T(8,128)S(1)}, s32[513,129]{0,1:T(8,128)}, u32[]{:S(2)}) copy-start(s32[513,129]{0,1:T(8,128)} %param.6) | copy-start | bytes 794128
  4.7 6.9 %copy-start.3 = (f32[16]{0:T(128)S(1)}, f32[16]{0:T(128)}, u32[]{:S(2)}) copy-start(f32[16]{0:T(128)} %param.5) | copy-start | bytes 196
  4.7 8.7 %copy-start.2 = (s32[513,129]{0,1:T(8,128)S(1)}, s32[513,129]{0,1:T(8,128)}, u32[]{:S(2)}) copy-start(s32[513,129]{0,1:T(8,128)} %param.7) | copy-start | bytes 794128
  4.7 30.5 %all-to-all-start = ((f32[64,16,256]{2,0,1:T(8,128)}), f32[64,16,256]{2,0,1:T(8,128)S(1)}, u32[]{:S(2)}, u32[]{:S(2)}) async-start(f32[64,16,256]{2,0,1:T(8,128)} %convolution_bitcast_fusion), calls=%async_computation | async-start | bytes 2097152 | tf_op jit(solution)/shard_map/all_to_all | solution.py:142
  46.0 10.5 %copy-start.4 = (f32[513,256]{0,1:T(8,128)}, f32[513,256]{0,1:T(8,128)S(1)}, u32[]{:S(2)}) copy-start(f32[513,256]{0,1:T(8,128)S(1)} %fusion.41) | copy-start | bytes 1575940
  83.3 29.7 %all-to-all-start.1 = ((f32[1024,1,256]{2,1,0:T(1,128)}), f32[1024,1,256]{2,1,0:T(1,128)S(1)}, u32[]{:S(2)}, u32[]{:S(2)}) async-start(f32[1024,1,256]{2,1,0:T(1,128)} %copy.43), calls=%async_computation.1 | async-start | bytes 2097152 | tf_op jit(solution)/shard_map/all_to_all | solution.py:163
  115.7 4.8 %collective-permute-start = (f32[1,16,256]{2,1,0:T(8,128)S(1)}, f32[1,16,256]{2,1,0:T(8,128)S(1)}, u32[]{:S(2)}, u32[]{:S(2)}) collective-permute-start(f32[1,16,256]{2,1,0:T(8,128)S(1)} %get-tuple-element.45), channel_id=1, source_target_pairs={{1,0},{2,1},{3,2},{4,3},{5,4},{6,5},{7,6},{8,7},{9,8},{10,9},{11,1... | collective-permute-start | bytes 49160 | tf_op jit(solution)/shard_map/ppermute | solution.py:25
  118.2 6.0 %collective-permute-start.1 = (f32[1,16,256]{2,1,0:T(8,128)S(1)}, f32[1,16,256]{2,1,0:T(8,128)S(1)}, u32[]{:S(2)}, u32[]{:S(2)}) collective-permute-start(f32[1,16,256]{2,1,0:T(8,128)S(1)} %get-tuple-element.46), channel_id=1, source_target_pairs={{0,1},{1,2},{2,3},{3,4},{4,5},{5,6},{6,7},{7,8},{8,9},{9,10},{10,1... | collective-permute-start | bytes 49160 | tf_op jit(solution)/shard_map/ppermute | solution.py:24
  125.5 5.1 %collective-permute-start.2 = (f32[1,16,256]{2,1,0:T(8,128)S(1)}, f32[1,16,256]{2,1,0:T(8,128)S(1)}, u32[]{:S(2)}, u32[]{:S(2)}) collective-permute-start(f32[1,16,256]{2,1,0:T(8,128)S(1)} %get-tuple-element.43), channel_id=1, source_target_pairs={{1,0},{2,1},{3,2},{4,3},{5,4},{6,5},{7,6},{8,7},{9,8},{10,9},{11,1... | collective-permute-start | bytes 49160 | tf_op jit(solution)/shard_map/ppermute | solution.py:25
  127.4 6.0 %collective-permute-start.3 = (f32[1,16,256]{2,1,0:T(8,128)S(1)}, f32[1,16,256]{2,1,0:T(8,128)S(1)}, u32[]{:S(2)}, u32[]{:S(2)}) collective-permute-start(f32[1,16,256]{2,1,0:T(8,128)S(1)} %get-tuple-element.44), channel_id=1, source_target_pairs={{0,1},{1,2},{2,3},{3,4},{4,5},{5,6},{6,7},{7,8},{8,9},{9,10},{10,1... | collective-permute-start | bytes 49160 | tf_op jit(solution)/shard_map/ppermute | solution.py:24
  134.3 4.3 %collective-permute-start.4 = (f32[1,16,256]{2,1,0:T(8,128)S(1)}, f32[1,16,256]{2,1,0:T(8,128)S(1)}, u32[]{:S(2)}, u32[]{:S(2)}) collective-permute-start(f32[1,16,256]{2,1,0:T(8,128)S(1)} %get-tuple-element.41), channel_id=1, source_target_pairs={{1,0},{2,1},{3,2},{4,3},{5,4},{6,5},{7,6},{8,7},{9,8},{10,9},{11,1... | collective-permute-start | bytes 49160 | tf_op jit(solution)/shard_map/ppermute | solution.py:25
  136.3 6.0 %collective-permute-start.5 = (f32[1,16,256]{2,1,0:T(8,128)S(1)}, f32[1,16,256]{2,1,0:T(8,128)S(1)}, u32[]{:S(2)}, u32[]{:S(2)}) collective-permute-start(f32[1,16,256]{2,1,0:T(8,128)S(1)} %get-tuple-element.42), channel_id=1, source_target_pairs={{0,1},{1,2},{2,3},{3,4},{4,5},{5,6},{6,7},{7,8},{8,9},{9,10},{10,1... | collective-permute-start | bytes 49160 | tf_op jit(solution)/shard_map/ppermute | solution.py:24
  143.8 4.8 %collective-permute-start.6 = (f32[1,16,256]{2,1,0:T(8,128)S(1)}, f32[1,16,256]{2,1,0:T(8,128)S(1)}, u32[]{:S(2)}, u32[]{:S(2)}) collective-permute-start(f32[1,16,256]{2,1,0:T(8,128)S(1)} %get-tuple-element.37), channel_id=1, source_target_pairs={{1,0},{2,1},{3,2},{4,3},{5,4},{6,5},{7,6},{8,7},{9,8},{10,9},{11,1... | collective-permute-start | bytes 49160 | tf_op jit(solution)/shard_map/ppermute | solution.py:25
  145.7 6.0 %collective-permute-start.7 = (f32[1,16,256]{2,1,0:T(8,128)S(1)}, f32[1,16,256]{2,1,0:T(8,128)S(1)}, u32[]{:S(2)}, u32[]{:S(2)}) collective-permute-start(f32[1,16,256]{2,1,0:T(8,128)S(1)} %get-tuple-element.38), channel_id=1, source_target_pairs={{0,1},{1,2},{2,3},{3,4},{4,5},{5,6},{6,7},{7,8},{8,9},{9,10},{10,1... | collective-permute-start | bytes 49160 | tf_op jit(solution)/shard_map/ppermute | solution.py:24
  155.3 30.2 %copy-start.5 = (f32[513,256]{0,1:T(8,128)S(1)}, f32[513,256]{0,1:T(8,128)}, u32[]{:S(2)}) copy-start(f32[513,256]{0,1:T(8,128)} %copy-done.4) | copy-start | bytes 1575940
  264.8 5.2 %collective-permute-start.8 = (f32[1,16,256]{2,1,0:T(8,128)S(1)}, f32[1,16,256]{2,1,0:T(8,128)S(1)}, u32[]{:S(2)}, u32[]{:S(2)}) collective-permute-start(f32[1,16,256]{2,1,0:T(8,128)S(1)} %get-tuple-element.35), channel_id=1, source_target_pairs={{1,0},{2,1},{3,2},{4,3},{5,4},{6,5},{7,6},{8,7},{9,8},{10,9},{11,1... | collective-permute-start | bytes 49160 | tf_op jit(solution)/shard_map/ppermute | solution.py:25
  268.1 6.0 %collective-permute-start.9 = (f32[1,16,256]{2,1,0:T(8,128)S(1)}, f32[1,16,256]{2,1,0:T(8,128)S(1)}, u32[]{:S(2)}, u32[]{:S(2)}) collective-permute-start(f32[1,16,256]{2,1,0:T(8,128)S(1)} %get-tuple-element.36), channel_id=1, source_target_pairs={{0,1},{1,2},{2,3},{3,4},{4,5},{5,6},{6,7},{7,8},{8,9},{9,10},{10,1... | collective-permute-start | bytes 49160 | tf_op jit(solution)/shard_map/ppermute | solution.py:24
  275.6 4.8 %collective-permute-start.10 = (f32[1,16,256]{2,1,0:T(8,128)S(1)}, f32[1,16,256]{2,1,0:T(8,128)S(1)}, u32[]{:S(2)}, u32[]{:S(2)}) collective-permute-start(f32[1,16,256]{2,1,0:T(8,128)S(1)} %get-tuple-element.31), channel_id=1, source_target_pairs={{1,0},{2,1},{3,2},{4,3},{5,4},{6,5},{7,6},{8,7},{9,8},{10,9},{11,1... | collective-permute-start | bytes 49160 | tf_op jit(solution)/shard_map/ppermute | solution.py:25
  277.6 6.0 %collective-permute-start.11 = (f32[1,16,256]{2,1,0:T(8,128)S(1)}, f32[1,16,256]{2,1,0:T(8,128)S(1)}, u32[]{:S(2)}, u32[]{:S(2)}) collective-permute-start(f32[1,16,256]{2,1,0:T(8,128)S(1)} %get-tuple-element.32), channel_id=1, source_target_pairs={{0,1},{1,2},{2,3},{3,4},{4,5},{5,6},{6,7},{7,8},{8,9},{9,10},{10,1... | collective-permute-start | bytes 49160 | tf_op jit(solution)/shard_map/ppermute | solution.py:24
  284.5 4.3 %collective-permute-start.12 = (f32[1,16,256]{2,1,0:T(8,128)S(1)}, f32[1,16,256]{2,1,0:T(8,128)S(1)}, u32[]{:S(2)}, u32[]{:S(2)}) collective-permute-start(f32[1,16,256]{2,1,0:T(8,128)S(1)} %get-tuple-element.29), channel_id=1, source_target_pairs={{1,0},{2,1},{3,2},{4,3},{5,4},{6,5},{7,6},{8,7},{9,8},{10,9},{11,1... | collective-permute-start | bytes 49160 | tf_op jit(solution)/shard_map/ppermute | solution.py:25
  286.4 6.0 %collective-permute-start.13 = (f32[1,16,256]{2,1,0:T(8,128)S(1)}, f32[1,16,256]{2,1,0:T(8,128)S(1)}, u32[]{:S(2)}, u32[]{:S(2)}) collective-permute-start(f32[1,16,256]{2,1,0:T(8,128)S(1)} %get-tuple-element.30), channel_id=1, source_target_pairs={{0,1},{1,2},{2,3},{3,4},{4,5},{5,6},{6,7},{7,8},{8,9},{9,10},{10,1... | collective-permute-start | bytes 49160 | tf_op jit(solution)/shard_map/ppermute | solution.py:24
  293.9 4.8 %collective-permute-start.14 = (f32[1,16,256]{2,1,0:T(8,128)S(1)}, f32[1,16,256]{2,1,0:T(8,128)S(1)}, u32[]{:S(2)}, u32[]{:S(2)}) collective-permute-start(f32[1,16,256]{2,1,0:T(8,128)S(1)} %get-tuple-element.25), channel_id=1, source_target_pairs={{1,0},{2,1},{3,2},{4,3},{5,4},{6,5},{7,6},{8,7},{9,8},{10,9},{11,1... | collective-permute-start | bytes 49160 | tf_op jit(solution)/shard_map/ppermute | solution.py:25
  295.9 6.0 %collective-permute-start.15 = (f32[1,16,256]{2,1,0:T(8,128)S(1)}, f32[1,16,256]{2,1,0:T(8,128)S(1)}, u32[]{:S(2)}, u32[]{:S(2)}) collective-permute-start(f32[1,16,256]{2,1,0:T(8,128)S(1)} %get-tuple-element.26), channel_id=1, source_target_pairs={{0,1},{1,2},{2,3},{3,4},{4,5},{5,6},{6,7},{7,8},{8,9},{9,10},{10,1... | collective-permute-start | bytes 49160 | tf_op jit(solution)/shard_map/ppermute | solution.py:24
where the time goes:
time: 307 us; the launch traced here: 304 us
  matrix products  103 us (34%)
  waiting for transfers between devices  72.6 us (24%)
  blocking collectives  59.7 us (19%)
  starting transfers between devices  48.4 us (16%)
  other arithmetic  14.8 us (5%)
  local copies, waits for them, and re-layouts  4.73 us (2%)
    all_to_all x1, blocking collectives, local(): lax.all_to_all(jnp.dot(current, forward_z, precision=highest), 'gy', spli...  30.2 us
    all_to_all x1, blocking collectives, local(): lax.all_to_all(merged, 'gy', split_axis=0, concat_axis=1, tiled=True)  29.5 us
    ppermute x8, waiting for transfers between devices, extended(): before = lax.ppermute(last, axis, up)  26.8 us
    dot_general x2, matrix products, x_inverse(): jnp.dot(sin_back, flat_imag, precision=highest)  24.8 us
    dot_general x2, matrix products, x_inverse(): jnp.dot(cos_back, flat_real, precision=highest)  24.4 us
    all_to_all x1, waiting for transfers between devices, local(): lax.all_to_all(merged, 'gy', split_axis=0, concat_axis=1, tiled=True)  24.1 us
    all_to_all x1, waiting for transfers between devices, local(): lax.all_to_all(packed, 'gy', split_axis=1, concat_axis=0, tiled=True)  21.7 us
    dot_general x2, matrix products, x_forward(): imag_part = jnp.dot(sin_table, flat, precision=highest).reshape(shape_out)  21.4 us
  transfers between devices with their start and end apart: 18, of which 10 were waited for; matrix products, arithmetic and copies ran while one was open for 1% of the time, Pallas kernels for 0%

commit v1 on v0

--- a/solution.py
+++ b/solution.py
@@ -12,6 +12,18 @@
 huber_eps = 0.05
 bound_dual = 0.5
 highest = lax.Precision.HIGHEST
+
+
+def split_up(x, dim, size):
+    shape = x.shape
+    tiles = x.reshape(*shape[:dim], size, shape[dim] // size, *shape[dim + 1 :])
+    return jnp.moveaxis(tiles, dim, 0)
+
+
+def joined_along(blocks, dim):
+    blocks = jnp.moveaxis(blocks, 0, dim)
+    shape = blocks.shape
+    return blocks.reshape(*shape[:dim], shape[dim] * shape[dim + 1], *shape[dim + 2 :])
 
 
 def extended(value, sides, width):
@@ -146,13 +158,15 @@
     duals = (jnp.zeros_like(observed), jnp.zeros_like(observed), jnp.zeros_like(observed))
     for outer in range(OUTER):
         if outer > 0:
-            again = lax.all_to_all(
-                jnp.dot(current, forward_z, precision=highest),
-                "gy",
-                split_axis=1,
-                concat_axis=0,
-                tiled=True,
-            )
+            value_2 = jnp.dot(current, forward_z, precision=highest)
+            size, index = (lax.axis_size("gy"), lax.axis_index("gy"))
+            blocks = split_up(value_2, 1, size)
+            outs = [blocks[index]]
+            for step in range(1, size):
+                sent = blocks[index ^ step]
+                outs.append(lax.ppermute(sent, "gy", [(i_2, i_2 ^ step) for i_2 in range(size)]))
+            blocks = jnp.stack(outs)[index ^ jnp.arange(size)]
+            again = joined_along(blocks, 0)
             prior_real, prior_imag = x_forward(again, cos_table, sin_table)
         merged = x_inverse(
             g_data * data_real + g_prior * prior_real,

time: 307 us -> 322 us (1.049)
  blocking collectives: 59.7 us -> 28.7 us
  starting transfers between devices: 48.4 us -> 65.9 us
  waiting for transfers between devices: 72.6 us -> 88.5 us
  local copies, waits for them, and re-layouts: 4.73 us -> 9.8 us
  other arithmetic: 14.8 us -> 19.1 us
    all_to_all x1 -> x0, blocking collectives: 30.2 us -> none  [local(): lax.all_to_all(jnp.dot(current, forward_z, precision=highest), 'gy', spli...]
    ppermute x0 -> x15, starting transfers between devices: none -> 17.2 us  [local(): lax.ppermute(sent, 'gy', [(i_2, i_2 ^ step) for i_2 in range(size)])]
    ppermute x0 -> x15, waiting for transfers between devices: none -> 16.3 us  [local(): lax.ppermute(sent, 'gy', [(i_2, i_2 ^ step) for i_2 in range(size)])]
    div x8, other arithmetic: 8.02 us -> 12.5 us  [denoise(): duals = (raised[0] / shrink, raised[1] / shrink, raised[2] / shrink)]
  transfers between devices with their start and end apart: 18 -> 33, of which waited for: 10 -> 18; matrix products, arithmetic and copies ran while one was open for 1% -> 1% of each run, Pallas kernels for 0% -> 0%
where the time goes in v1:
time: 322 us; the launch traced here: 318 us
  matrix products  105 us (33%)
  waiting for transfers between devices  88.5 us (27%)
  starting transfers between devices  65.9 us (20%)
  blocking collectives  28.7 us (9%)
  other arithmetic  19.1 us (6%)
  local copies, waits for them, and re-layouts  9.8 us (3%)
    all_to_all x1, blocking collectives, local(): lax.all_to_all(merged, 'gy', split_axis=0, concat_axis=1, tiled=True)  28.7 us
    ppermute x8, waiting for transfers between devices, extended(): before = lax.ppermute(last, axis, up)  26.1 us
    dot_general x2, matrix products, x_inverse(): jnp.dot(sin_back, flat_imag, precision=highest)  24.8 us
    dot_general x2, matrix products, x_inverse(): jnp.dot(cos_back, flat_real, precision=highest)  24.2 us
    all_to_all x1, waiting for transfers between devices, local(): lax.all_to_all(merged, 'gy', split_axis=0, concat_axis=1, tiled=True)  24.1 us
    dot_general x2, matrix products, x_forward(): real_part = jnp.dot(cos_table, flat, precision=highest).reshape(shape_out)  23 us
    all_to_all x1, waiting for transfers between devices, local(): lax.all_to_all(packed, 'gy', split_axis=1, concat_axis=0, tiled=True)  22 us
    dot_general x2, matrix products, x_forward(): imag_part = jnp.dot(sin_table, flat, precision=highest).reshape(shape_out)  21.8 us
  transfers between devices with their start and end apart: 33, of which 18 were waited for; matrix products, arithmetic and copies ran while one was open for 1% of the time, Pallas kernels for 0%

profile of v1, /device:TPU:8, one launch (start us, length us, event | category | flops | bytes accessed | tf_op | source)
XLA Modules:
  0.0 318.1 jit_solution(4752081651464430529)
XLA Ops:
  1.2 3.4 %convolution_bitcast_fusion = f32[64,16,256]{2,0,1:T(8,128)} fusion(f32[64,16,256]{2,1,0:T(8,128)S(1)} %copy-done, s32[256]{0:T(256)S(1)} %add_select_fusion.3, pred[256]{0:T(512)(128)(4,1)S(1)} %iota_compare_fusion.3), kind=kOutput, calls=%fused_computation.56 | convolution fusion | flops 806289408 | bytes 2098432 | tf_op jit(solution)/shard_map/dot_general | solution.py:153
  4.7 6.6 %all-to-all-start = ((f32[64,16,256]{2,0,1:T(8,128)}), f32[64,16,256]{2,0,1:T(8,128)S(1)}, u32[]{:S(2)}, u32[]{:S(2)}) async-start(f32[64,16,256]{2,0,1:T(8,128)} %convolution_bitcast_fusion), calls=%async_computation | async-start | bytes 2097152 | tf_op jit(solution)/shard_map/all_to_all | solution.py:154
  13.2 22.0 %all-to-all-done = f32[64,16,256]{2,0,1:T(8,128)S(1)} async-done(((f32[64,16,256]{2,0,1:T(8,128)}), f32[64,16,256]{2,0,1:T(8,128)S(1)}, u32[]{:S(2)}, u32[]{:S(2)}) %all-to-all-start) | async-done | bytes 1048608 | tf_op jit(solution)/shard_map/all_to_all | solution.py:154
  35.2 10.9 %fusion.41 = f32[513,256]{0,1:T(8,128)S(1)} fusion(f32[1024,256]{1,0:T(8,128)S(1)} %bitcast.82), kind=kOutput, calls=%fused_computation.68 | convolution fusion | flops 1621112832 | bytes 1573888 | tf_op jit(solution)/shard_map/dot_general | solution.py:117
  46.1 10.7 %fusion.36 = f32[513,256]{0,1:T(8,128)S(1)} fusion(f32[1024,256]{1,0:T(8,128)S(1)} %bitcast.83), kind=kOutput, calls=%fused_computation.67 | convolution fusion | flops 1621112832 | bytes 1573888 | tf_op jit(solution)/shard_map/dot_general | solution.py:116
  56.8 12.5 %fusion.8 = f32[1024,256]{1,0:T(8,128)S(1)} fusion(f32[513]{0:T(1024)S(1)} %select_multiply_fusion.3, f32[513,256]{0,1:T(8,128)S(1)} %fusion.41, f32[513,127]{0,1:T(8,128)S(1)} %slice.278, f32[513,129]{0,1:T(8,128)S(1)} %convert_multiply_fusion), kind=kOutput, calls=%fused_computation.14 | convolution fusion | flops 1622688768 | bytes 2101252 | tf_op jit(solution)/shard_map/dot_general | solution.py:125
  69.4 12.1 %fusion.17 = f32[1024,1,256]{2,0,1:T(8,128)S(1)} fusion(f32[1024,256]{1,0:T(8,128)S(1)} %fusion.8, f32[513]{0:T(1024)S(1)} %select_multiply_fusion.3, f32[513,256]{0,1:T(8,128)S(1)} %fusion.36, f32[513,127]{0,1:T(8,128)S(1)} %slice.278, f32[513,129]{0,1:T(8,128)S(1)} %convert_multiply_fusion), kind=kOutput, calls=%fused_computation.53 | convolution fusion | flops 1622950912 | bytes 3149828 | tf_op jit(solution)/shard_map/dot_general | solution.py:125
  81.5 2.0 copy.34
  83.5 5.6 %all-to-all-start.1 = ((f32[1024,1,256]{2,1,0:T(1,128)}), f32[1024,1,256]{2,1,0:T(1,128)S(1)}, u32[]{:S(2)}, u32[]{:S(2)}) async-start(f32[1024,1,256]{2,1,0:T(1,128)} %copy.34), calls=%async_computation.1 | async-start | bytes 2097152 | tf_op jit(solution)/shard_map/all_to_all | solution.py:177
  89.2 24.1 %all-to-all-done.1 = f32[1024,1,256]{2,1,0:T(1,128)S(1)} async-done(((f32[1024,1,256]{2,1,0:T(1,128)}), f32[1024,1,256]{2,1,0:T(1,128)S(1)}, u32[]{:S(2)}, u32[]{:S(2)}) %all-to-all-start.1) | async-done | bytes 1048608 | tf_op jit(solution)/shard_map/all_to_all | solution.py:177
  113.3 2.6 fusion.152
  115.9 2.5 collective-permute-start
  118.5 2.3 collective-permute-start.1
  120.8 3.7 %collective-permute-done.1 = f32[1,16,256]{2,1,0:T(8,128)S(1)} collective-permute-done((f32[1,16,256]{2,1,0:T(8,128)S(1)}, f32[1,16,256]{2,1,0:T(8,128)S(1)}, u32[]{:S(2)}, u32[]{:S(2)}) %collective-permute-start.1) | collective-permute-done | bytes 16416 | tf_op jit(solution)/shard_map/ppermute | solution.py:36
  125.7 1.9 collective-permute-start.2
  127.7 2.4 collective-permute-start.3
  130.9 2.7 collective-permute-done.3
  139.0 2.4 collective-permute-start.5
  141.6 3.4 %collective-permute-done.5 = f32[1,16,256]{2,1,0:T(8,128)S(1)} collective-permute-done((f32[1,16,256]{2,1,0:T(8,128)S(1)}, f32[1,16,256]{2,1,0:T(8,128)S(1)}, u32[]{:S(2)}, u32[]{:S(2)}) %collective-permute-start.5) | collective-permute-done | bytes 16416 | tf_op jit(solution)/shard_map/ppermute | solution.py:36
  145.0 6.1 %fusion.256 = (f32[64,16,256]{2,1,0:T(8,128)S(1)}, f32[64,16,256]{2,1,0:T(8,128)S(1)}, f32[64,16,256]{2,1,0:T(8,128)S(1)}, f32[64,16,256]{2,1,0:T(8,128)S(1)}) fusion(f32[64,16,256]{2,1,0:T(8,128)S(1)} %get-tuple-element.21, f32[64,16,256]{2,1,0:T(8,128)} %copy-done.3, f32[1,16,256]{2,1,0:T(8,128)S(1)} %collective-permute-done.5, ...), kind=kLoop, calls=%fused_computation.347 | loop fusion | flops 6815744 | bytes 8421376 | tf_op jit(solution)/shard_map/div | solution.py:73
  151.1 1.9 collective-permute-start.6
  153.0 2.8 collective-permute-start.7
  156.2 2.7 collective-permute-done.7
  159.0 2.7 fusion.77
  162.9 2.1 collective-permute-start.9
  169.7 2.1 collective-permute-start.15
  172.2 3.5 %collective-permute-start.17 = (f32[64,1,256]{2,1,0:T(1,128)S(1)}, f32[64,1,256]{2,1,0:T(1,128)S(1)}, u32[]{:S(2)}, u32[]{:S(2)}) collective-permute-start(f32[64,1,256]{2,1,0:T(1,128)S(1)} %get-tuple-element.42), channel_id=1, source_target_pairs={{0,10},{1,11},{2,8},{3,9},{4,14},{5,15},{6,12},{7,13},{8,2},{9,3},... | collective-permute-start | bytes 196616 | tf_op jit(solution)/shard_map/ppermute | solution.py:167
  176.2 2.6 collective-permute-start.19
  179.8 3.6 %collective-permute-done.16 = f32[64,1,256]{2,1,0:T(1,128)S(1)} collective-permute-done((f32[64,1,256]{2,1,0:T(1,128)S(1)}, f32[64,1,256]{2,1,0:T(1,128)S(1)}, u32[]{:S(2)}, u32[]{:S(2)}) %collective-permute-start.16) | collective-permute-done | bytes 65568 | tf_op jit(solution)/shard_map/ppermute | solution.py:167
  186.9 4.1 %collective-permute-done.19 = f32[64,1,256]{2,1,0:T(1,128)S(1)} collective-permute-done((f32[64,1,256]{2,1,0:T(1,128)S(1)}, f32[64,1,256]{2,1,0:T(1,128)S(1)}, u32[]{:S(2)}, u32[]{:S(2)}) %collective-permute-start.19) | collective-permute-done | bytes 65568 | tf_op jit(solution)/shard_map/ppermute | solution.py:167
  192.4 2.8 collective-permute-done.21
  198.4 12.3 %fusion.27 = f32[513,256]{0,1:T(8,128)S(1)} fusion(f32[1024,256]{1,0:T(8,128)} %bitcast.80, f32[513,256]{0,1:T(8,128)} %copy-done.21, f32[513,127]{0,1:T(8,128)} %copy-done.12, f32[513,129]{0,1:T(8,128)S(1)} %convert_multiply_fusion), kind=kOutput, calls=%fused_computation.60 | convolution fusion | flops 1622163456 | bytes 2624512 | tf_op jit(solution)/shard_map/dot_general | solution.py:116
  210.7 10.8 %fusion.26 = f32[513,256]{0,1:T(8,128)S(1)} fusion(f32[1024,256]{1,0:T(8,128)S(1)} %bitcast.81, f32[513,256]{0,1:T(8,128)S(1)} %copy-done.20, f32[513,127]{0,1:T(8,128)S(1)} %copy-done.13, f32[513,129]{0,1:T(8,128)S(1)} %convert_multiply_fusion), kind=kOutput, calls=%fused_computation.58 | convolution fusion | flops 1622163456 | bytes 2624512 | tf_op jit(solution)/shard_map/dot_general | solution.py:117
  221.6 12.3 %fusion.6 = f32[1024,256]{1,0:T(8,128)S(1)} fusion(f32[513,256]{0,1:T(8,128)S(1)} %fusion.26, f32[513]{0:T(1024)S(1)} %copy-done.17), kind=kOutput, calls=%fused_computation.12 | convolution fusion | flops 1621638144 | bytes 1575940 | tf_op jit(solution)/shard_map/dot_general | solution.py:125
  233.9 12.1 %fusion.23 = f32[1024,1,256]{2,0,1:T(8,128)S(1)} fusion(f32[1024,256]{1,0:T(8,128)S(1)} %fusion.6, f32[513,256]{0,1:T(8,128)S(1)} %fusion.27, f32[513]{0:T(1024)S(1)} %copy-done.17), kind=kOutput, calls=%fused_computation.55 | convolution fusion | flops 1621900288 | bytes 2624516 | tf_op jit(solution)/shard_map/dot_general | solution.py:125
  247.1 28.7 %all_to_all.51 = f32[1024,1,256]{2,1,0:T(1,128)S(1)} all-to-all(f32[1024,1,256]{2,1,0:T(1,128)S(1)} %copy.38), channel_id=1, replica_groups=mesh['groups'=2,'gy'=16] {'gy'}, dimensions={0} | all-to-all | bytes 2097152 | tf_op jit(solution)/shard_map/all_to_all | solution.py:177
  276.4 2.6 fusion.150
  279.0 3.2 %collective-permute-start.23 = (f32[1,16,256]{2,1,0:T(8,128)S(1)}, f32[1,16,256]{2,1,0:T(8,128)S(1)}, u32[]{:S(2)}, u32[]{:S(2)}) collective-permute-start(f32[1,16,256]{2,1,0:T(8,128)S(1)} %get-tuple-element.35), channel_id=1, source_target_pairs={{1,0},{2,1},{3,2},{4,3},{5,4},{6,5},{7,6},{8,7},{9,8},{10,9},{11,1... | collective-permute-start | bytes 49160 | tf_op jit(solution)/shard_map/ppermute | solution.py:37
  282.3 1.9 collective-permute-start.24
  284.2 4.0 %collective-permute-done.24 = f32[1,16,256]{2,1,0:T(8,128)S(1)} collective-permute-done((f32[1,16,256]{2,1,0:T(8,128)S(1)}, f32[1,16,256]{2,1,0:T(8,128)S(1)}, u32[]{:S(2)}, u32[]{:S(2)}) %collective-permute-start.24) | collective-permute-done | bytes 16416 | tf_op jit(solution)/shard_map/ppermute | solution.py:36
  289.8 1.9 collective-permute-start.25
  291.7 2.6 collective-permute-start.26
  294.8 2.9 collective-permute-done.26
  300.6 2.4 collective-permute-start.28
  303.0 3.5 %collective-permute-done.28 = f32[1,16,256]{2,1,0:T(8,128)S(1)} collective-permute-done((f32[1,16,256]{2,1,0:T(8,128)S(1)}, f32[1,16,256]{2,1,0:T(8,128)S(1)}, u32[]{:S(2)}, u32[]{:S(2)}) %collective-permute-start.28) | collective-permute-done | bytes 16416 | tf_op jit(solution)/shard_map/ppermute | solution.py:36
  310.0 2.4 collective-permute-start.30
  312.9 3.1 collective-permute-done.30
  316.0 1.9 fusion.118
  (126 shorter events, 37.2 us)
Async XLA Ops:
  4.7 6.6 %copy-start.10 = (s32[513,129]{0,1:T(8,128)S(1)}, s32[513,129]{0,1:T(8,128)}, u32[]{:S(2)}) copy-start(s32[513,129]{0,1:T(8,128)} %param.6) | copy-start | bytes 794128
  4.7 6.6 %copy-start.18 = (f32[16]{0:T(128)S(1)}, f32[16]{0:T(128)}, u32[]{:S(2)}) copy-start(f32[16]{0:T(128)} %param.5) | copy-start | bytes 196
  4.7 8.4 %copy-start.11 = (s32[513,129]{0,1:T(8,128)S(1)}, s32[513,129]{0,1:T(8,128)}, u32[]{:S(2)}) copy-start(s32[513,129]{0,1:T(8,128)} %param.7) | copy-start | bytes 794128
  4.7 30.5 %all-to-all-start = ((f32[64,16,256]{2,0,1:T(8,128)}), f32[64,16,256]{2,0,1:T(8,128)S(1)}, u32[]{:S(2)}, u32[]{:S(2)}) async-start(f32[64,16,256]{2,0,1:T(8,128)} %convolution_bitcast_fusion), calls=%async_computation | async-start | bytes 2097152 | tf_op jit(solution)/shard_map/all_to_all | solution.py:154
  13.2 56.2 %copy-start.12 = (f32[513,127]{0,1:T(8,128)}, f32[513,127]{0,1:T(8,128)S(1)}, u32[]{:S(2)}) copy-start(f32[513,127]{0,1:T(8,128)S(1)} %slice.278) | copy-start | bytes 781816
  13.2 56.2 %copy-start.16 = (f32[513]{0:T(1024)}, f32[513]{0:T(1024)S(1)}, u32[]{:S(2)}) copy-start(f32[513]{0:T(1024)S(1)} %select_multiply_fusion.3) | copy-start | bytes 6160
  46.1 10.7 %copy-start.19 = (f32[513,256]{0,1:T(8,128)}, f32[513,256]{0,1:T(8,128)S(1)}, u32[]{:S(2)}) copy-start(f32[513,256]{0,1:T(8,128)S(1)} %fusion.41) | copy-start | bytes 1575940
  56.8 12.6 %copy-start.21 = (f32[513,256]{0,1:T(8,128)}, f32[513,256]{0,1:T(8,128)S(1)}, u32[]{:S(2)}) copy-start(f32[513,256]{0,1:T(8,128)S(1)} %fusion.36) | copy-start | bytes 1575940
  83.5 29.7 %all-to-all-start.1 = ((f32[1024,1,256]{2,1,0:T(1,128)}), f32[1024,1,256]{2,1,0:T(1,128)S(1)}, u32[]{:S(2)}, u32[]{:S(2)}) async-start(f32[1024,1,256]{2,1,0:T(1,128)} %copy.34), calls=%async_computation.1 | async-start | bytes 2097152 | tf_op jit(solution)/shard_map/all_to_all | solution.py:177
  89.2 24.1 %copy-start.14 = (f32[256]{0:T(256)}, f32[256]{0:T(256)S(1)}, u32[]{:S(2)}) copy-start(f32[256]{0:T(256)S(1)} %fusion.205) | copy-start | bytes 3076
  115.9 4.8 %collective-permute-start = (f32[1,16,256]{2,1,0:T(8,128)S(1)}, f32[1,16,256]{2,1,0:T(8,128)S(1)}, u32[]{:S(2)}, u32[]{:S(2)}) collective-permute-start(f32[1,16,256]{2,1,0:T(8,128)S(1)} %get-tuple-element.60), channel_id=1, source_target_pairs={{1,0},{2,1},{3,2},{4,3},{5,4},{6,5},{7,6},{8,7},{9,8},{10,9},{11,1... | collective-permute-start | bytes 49160 | tf_op jit(solution)/shard_map/ppermute | solution.py:37
  118.5 6.0 %collective-permute-start.1 = (f32[1,16,256]{2,1,0:T(8,128)S(1)}, f32[1,16,256]{2,1,0:T(8,128)S(1)}, u32[]{:S(2)}, u32[]{:S(2)}) collective-permute-start(f32[1,16,256]{2,1,0:T(8,128)S(1)} %get-tuple-element.61), channel_id=1, source_target_pairs={{0,1},{1,2},{2,3},{3,4},{4,5},{5,6},{6,7},{7,8},{8,9},{9,10},{10,1... | collective-permute-start | bytes 49160 | tf_op jit(solution)/shard_map/ppermute | solution.py:36
  125.7 5.2 %collective-permute-start.2 = (f32[1,16,256]{2,1,0:T(8,128)S(1)}, f32[1,16,256]{2,1,0:T(8,128)S(1)}, u32[]{:S(2)}, u32[]{:S(2)}) collective-permute-start(f32[1,16,256]{2,1,0:T(8,128)S(1)} %get-tuple-element.58), channel_id=1, source_target_pairs={{1,0},{2,1},{3,2},{4,3},{5,4},{6,5},{7,6},{8,7},{9,8},{10,9},{11,1... | collective-permute-start | bytes 49160 | tf_op jit(solution)/shard_map/ppermute | solution.py:37
  127.7 6.0 %collective-permute-start.3 = (f32[1,16,256]{2,1,0:T(8,128)S(1)}, f32[1,16,256]{2,1,0:T(8,128)S(1)}, u32[]{:S(2)}, u32[]{:S(2)}) collective-permute-start(f32[1,16,256]{2,1,0:T(8,128)S(1)} %get-tuple-element.59), channel_id=1, source_target_pairs={{0,1},{1,2},{2,3},{3,4},{4,5},{5,6},{6,7},{7,8},{8,9},{9,10},{10,1... | collective-permute-start | bytes 49160 | tf_op jit(solution)/shard_map/ppermute | solution.py:36
  137.1 4.4 %collective-permute-start.4 = (f32[1,16,256]{2,1,0:T(8,128)}, f32[1,16,256]{2,1,0:T(8,128)S(1)}, u32[]{:S(2)}, u32[]{:S(2)}) collective-permute-start(f32[1,16,256]{2,1,0:T(8,128)} %get-tuple-element.56), channel_id=1, source_target_pairs={{1,0},{2,1},{3,2},{4,3},{5,4},{6,5},{7,6},{8,7},{9,8},{10,9},{11,1... | collective-permute-start | bytes 49160 | tf_op jit(solution)/shard_map/ppermute | solution.py:37
  139.0 6.0 %collective-permute-start.5 = (f32[1,16,256]{2,1,0:T(8,128)S(1)}, f32[1,16,256]{2,1,0:T(8,128)S(1)}, u32[]{:S(2)}, u32[]{:S(2)}) collective-permute-start(f32[1,16,256]{2,1,0:T(8,128)S(1)} %get-tuple-element.57), channel_id=1, source_target_pairs={{0,1},{1,2},{2,3},{3,4},{4,5},{5,6},{6,7},{7,8},{8,9},{9,10},{10,1... | collective-permute-start | bytes 49160 | tf_op jit(solution)/shard_map/ppermute | solution.py:36
  151.1 7.9 %copy-start.4 = (f32[64,16,256]{2,1,0:T(8,128)}, f32[64,16,256]{2,1,0:T(8,128)S(1)}, u32[]{:S(2)}) copy-start(f32[64,16,256]{2,1,0:T(8,128)S(1)} %get-tuple-element.15) | copy-start | bytes 3145732
  151.1 5.1 %collective-permute-start.6 = (f32[1,16,256]{2,1,0:T(8,128)S(1)}, f32[1,16,256]{2,1,0:T(8,128)S(1)}, u32[]{:S(2)}, u32[]{:S(2)}) collective-permute-start(f32[1,16,256]{2,1,0:T(8,128)S(1)} %get-tuple-element.52), channel_id=1, source_target_pairs={{1,0},{2,1},{3,2},{4,3},{5,4},{6,5},{7,6},{8,7},{9,8},{10,9},{11,1... | collective-permute-start | bytes 49160 | tf_op jit(solution)/shard_map/ppermute | solution.py:37
  153.0 6.0 %collective-permute-start.7 = (f32[1,16,256]{2,1,0:T(8,128)S(1)}, f32[1,16,256]{2,1,0:T(8,128)S(1)}, u32[]{:S(2)}, u32[]{:S(2)}) collective-permute-start(f32[1,16,256]{2,1,0:T(8,128)S(1)} %get-tuple-element.53), channel_id=1, source_target_pairs={{0,1},{1,2},{2,3},{3,4},{4,5},{5,6},{6,7},{7,8},{8,9},{9,10},{10,1... | collective-permute-start | bytes 49160 | tf_op jit(solution)/shard_map/ppermute | solution.py:36
  162.9 3.7 %collective-permute-start.8 = (f32[64,1,256]{2,1,0:T(1,128)S(1)}, f32[64,1,256]{2,1,0:T(1,128)S(1)}, u32[]{:S(2)}, u32[]{:S(2)}) collective-permute-start(f32[64,1,256]{2,1,0:T(1,128)S(1)} %get-tuple-element.51), channel_id=1, source_target_pairs={{0,1},{1,0},{2,3},{3,2},{4,5},{5,4},{6,7},{7,6},{8,9},{9,8},{10,11... | collective-permute-start | bytes 196616 | tf_op jit(solution)/shard_map/ppermute | solution.py:167
  162.9 5.5 %collective-permute-start.9 = (f32[64,1,256]{2,1,0:T(1,128)S(1)}, f32[64,1,256]{2,1,0:T(1,128)S(1)}, u32[]{:S(2)}, u32[]{:S(2)}) collective-permute-start(f32[64,1,256]{2,1,0:T(1,128)S(1)} %get-tuple-element.50), channel_id=1, source_target_pairs={{0,2},{1,3},{2,0},{3,1},{4,6},{5,7},{6,4},{7,5},{8,10},{9,11},{10,... | collective-permute-start | bytes 196616 | tf_op jit(solution)/shard_map/ppermute | solution.py:167
  165.0 4.6 %collective-permute-start.10 = (f32[64,1,256]{2,1,0:T(1,128)S(1)}, f32[64,1,256]{2,1,0:T(1,128)S(1)}, u32[]{:S(2)}, u32[]{:S(2)}) collective-permute-start(f32[64,1,256]{2,1,0:T(1,128)S(1)} %get-tuple-element.49), channel_id=1, source_target_pairs={{0,3},{1,2},{2,1},{3,0},{4,7},{5,6},{6,5},{7,4},{8,11},{9,10},{10,... | collective-permute-start | bytes 196616 | tf_op jit(solution)/shard_map/ppermute | solution.py:167
  165.0 6.7 %collective-permute-start.11 = (f32[64,1,256]{2,1,0:T(1,128)S(1)}, f32[64,1,256]{2,1,0:T(1,128)S(1)}, u32[]{:S(2)}, u32[]{:S(2)}) collective-permute-start(f32[64,1,256]{2,1,0:T(1,128)S(1)} %get-tuple-element.48), channel_id=1, source_target_pairs={{0,4},{1,5},{2,6},{3,7},{4,0},{5,1},{6,2},{7,3},{8,12},{9,13},{10,... | collective-permute-start | bytes 196616 | tf_op jit(solution)/shard_map/ppermute | solution.py:167
  165.0 7.2 %collective-permute-start.12 = (f32[64,1,256]{2,1,0:T(1,128)S(1)}, f32[64,1,256]{2,1,0:T(1,128)S(1)}, u32[]{:S(2)}, u32[]{:S(2)}) collective-permute-start(f32[64,1,256]{2,1,0:T(1,128)S(1)} %get-tuple-element.47), channel_id=1, source_target_pairs={{0,5},{1,4},{2,7},{3,6},{4,1},{5,0},{6,3},{7,2},{8,13},{9,12},{10,... | collective-permute-start | bytes 196616 | tf_op jit(solution)/shard_map/ppermute | solution.py:167
  166.6 9.2 %collective-permute-start.13 = (f32[64,1,256]{2,1,0:T(1,128)S(1)}, f32[64,1,256]{2,1,0:T(1,128)S(1)}, u32[]{:S(2)}, u32[]{:S(2)}) collective-permute-start(f32[64,1,256]{2,1,0:T(1,128)S(1)} %get-tuple-element.46), channel_id=1, source_target_pairs={{0,6},{1,7},{2,4},{3,5},{4,2},{5,3},{6,0},{7,1},{8,14},{9,15},{10,... | collective-permute-start | bytes 196616 | tf_op jit(solution)/shard_map/ppermute | solution.py:167
  168.4 7.8 %collective-permute-start.14 = (f32[64,1,256]{2,1,0:T(1,128)S(1)}, f32[64,1,256]{2,1,0:T(1,128)S(1)}, u32[]{:S(2)}, u32[]{:S(2)}) collective-permute-start(f32[64,1,256]{2,1,0:T(1,128)S(1)} %get-tuple-element.45), channel_id=1, source_target_pairs={{0,7},{1,6},{2,5},{3,4},{4,3},{5,2},{6,1},{7,0},{8,15},{9,14},{10,... | collective-permute-start | bytes 196616 | tf_op jit(solution)/shard_map/ppermute | solution.py:167
  169.7 10.1 %collective-permute-start.15 = (f32[64,1,256]{2,1,0:T(1,128)S(1)}, f32[64,1,256]{2,1,0:T(1,128)S(1)}, u32[]{:S(2)}, u32[]{:S(2)}) collective-permute-start(f32[64,1,256]{2,1,0:T(1,128)S(1)} %get-tuple-element.44), channel_id=1, source_target_pairs={{0,8},{1,9},{2,10},{3,11},{4,12},{5,13},{6,14},{7,15},{8,0},{9,1},... | collective-permute-start | bytes 196616 | tf_op jit(solution)/shard_map/ppermute | solution.py:167
  171.8 11.6 %collective-permute-start.16 = (f32[64,1,256]{2,1,0:T(1,128)S(1)}, f32[64,1,256]{2,1,0:T(1,128)S(1)}, u32[]{:S(2)}, u32[]{:S(2)}) collective-permute-start(f32[64,1,256]{2,1,0:T(1,128)S(1)} %get-tuple-element.43), channel_id=1, source_target_pairs={{0,9},{1,8},{2,11},{3,10},{4,13},{5,12},{6,15},{7,14},{8,1},{9,0},... | collective-permute-start | bytes 196616 | tf_op jit(solution)/shard_map/ppermute | solution.py:167
  172.2 12.7 %collective-permute-start.17 = (f32[64,1,256]{2,1,0:T(1,128)S(1)}, f32[64,1,256]{2,1,0:T(1,128)S(1)}, u32[]{:S(2)}, u32[]{:S(2)}) collective-permute-start(f32[64,1,256]{2,1,0:T(1,128)S(1)} %get-tuple-element.42), channel_id=1, source_target_pairs={{0,10},{1,11},{2,8},{3,9},{4,14},{5,15},{6,12},{7,13},{8,2},{9,3},... | collective-permute-start | bytes 196616 | tf_op jit(solution)/shard_map/ppermute | solution.py:167
  175.8 11.1 %collective-permute-start.18 = (f32[64,1,256]{2,1,0:T(1,128)S(1)}, f32[64,1,256]{2,1,0:T(1,128)S(1)}, u32[]{:S(2)}, u32[]{:S(2)}) collective-permute-start(f32[64,1,256]{2,1,0:T(1,128)S(1)} %get-tuple-element.41), channel_id=1, source_target_pairs={{0,11},{1,10},{2,9},{3,8},{4,15},{5,14},{6,13},{7,12},{8,3},{9,2},... | collective-permute-start | bytes 196616 | tf_op jit(solution)/shard_map/ppermute | solution.py:167
  176.2 14.8 %collective-permute-start.19 = (f32[64,1,256]{2,1,0:T(1,128)S(1)}, f32[64,1,256]{2,1,0:T(1,128)S(1)}, u32[]{:S(2)}, u32[]{:S(2)}) collective-permute-start(f32[64,1,256]{2,1,0:T(1,128)S(1)} %get-tuple-element.40), channel_id=1, source_target_pairs={{0,12},{1,13},{2,14},{3,15},{4,8},{5,9},{6,10},{7,11},{8,4},{9,5},... | collective-permute-start | bytes 196616 | tf_op jit(solution)/shard_map/ppermute | solution.py:167
  179.7 12.7 %collective-permute-start.20 = (f32[64,1,256]{2,1,0:T(1,128)S(1)}, f32[64,1,256]{2,1,0:T(1,128)S(1)}, u32[]{:S(2)}, u32[]{:S(2)}) collective-permute-start(f32[64,1,256]{2,1,0:T(1,128)S(1)} %get-tuple-element.39), channel_id=1, source_target_pairs={{0,13},{1,12},{2,15},{3,14},{4,9},{5,8},{6,11},{7,10},{8,5},{9,4},... | collective-permute-start | bytes 196616 | tf_op jit(solution)/shard_map/ppermute | solution.py:167
  183.4 11.9 %collective-permute-start.21 = (f32[64,1,256]{2,1,0:T(1,128)S(1)}, f32[64,1,256]{2,1,0:T(1,128)S(1)}, u32[]{:S(2)}, u32[]{:S(2)}) collective-permute-start(f32[64,1,256]{2,1,0:T(1,128)S(1)} %get-tuple-element.38), channel_id=1, source_target_pairs={{0,14},{1,15},{2,12},{3,13},{4,10},{5,11},{6,8},{7,9},{8,6},{9,7},... | collective-permute-start | bytes 196616 | tf_op jit(solution)/shard_map/ppermute | solution.py:167
  184.9 11.8 %collective-permute-start.22 = (f32[64,1,256]{2,1,0:T(1,128)S(1)}, f32[64,1,256]{2,1,0:T(1,128)S(1)}, u32[]{:S(2)}, u32[]{:S(2)}) collective-permute-start(f32[64,1,256]{2,1,0:T(1,128)S(1)} %get-tuple-element.37), channel_id=1, source_target_pairs={{0,15},{1,14},{2,13},{3,12},{4,11},{5,10},{6,9},{7,8},{8,7},{9,6},... | collective-permute-start | bytes 196616 | tf_op jit(solution)/shard_map/ppermute | solution.py:167
  198.4 12.3 %copy-start.8 = (f32[16,64,256]{2,1,0:T(8,128)S(1)}, f32[16,64,256]{2,1,0:T(8,128)}, u32[]{:S(2)}) copy-start(f32[16,64,256]{2,1,0:T(8,128)} %gather_fusion) | copy-start | bytes 3145732
  198.4 12.4 %copy-start.13 = (f32[513,127]{0,1:T(8,128)S(1)}, f32[513,127]{0,1:T(8,128)}, u32[]{:S(2)}) copy-start(f32[513,127]{0,1:T(8,128)} %copy-done.12) | copy-start | bytes 781816
  198.4 12.4 %copy-start.20 = (f32[513,256]{0,1:T(8,128)S(1)}, f32[513,256]{0,1:T(8,128)}, u32[]{:S(2)}) copy-start(f32[513,256]{0,1:T(8,128)} %copy-done.19) | copy-start | bytes 1575940
  210.7 10.8 %copy-start.17 = (f32[513]{0:T(1024)S(1)}, f32[513]{0:T(1024)}, u32[]{:S(2)}) copy-start(f32[513]{0:T(1024)} %copy-done.16) | copy-start | bytes 6160
  276.4 11.8 %copy-start.5 = (f32[64,16,256]{2,1,0:T(8,128)S(1)}, f32[64,16,256]{2,1,0:T(8,128)}, u32[]{:S(2)}) copy-start(f32[64,16,256]{2,1,0:T(8,128)} %copy-done.4) | copy-start | bytes 3145732
  276.4 11.8 %copy-start.7 = (f32[64,16,256]{2,1,0:T(8,128)S(1)}, f32[64,16,256]{2,1,0:T(8,128)}, u32[]{:S(2)}) copy-start(f32[64,16,256]{2,1,0:T(8,128)} %copy-done.6) | copy-start | bytes 3145732
  279.0 5.2 %collective-permute-start.23 = (f32[1,16,256]{2,1,0:T(8,128)S(1)}, f32[1,16,256]{2,1,0:T(8,128)S(1)}, u32[]{:S(2)}, u32[]{:S(2)}) collective-permute-start(f32[1,16,256]{2,1,0:T(8,128)S(1)} %get-tuple-element.35), channel_id=1, source_target_pairs={{1,0},{2,1},{3,2},{4,3},{5,4},{6,5},{7,6},{8,7},{9,8},{10,9},{11,1... | collective-permute-start | bytes 49160 | tf_op jit(solution)/shard_map/ppermute | solution.py:37
  282.3 6.0 %collective-permute-start.24 = (f32[1,16,256]{2,1,0:T(8,128)S(1)}, f32[1,16,256]{2,1,0:T(8,128)S(1)}, u32[]{:S(2)}, u32[]{:S(2)}) collective-permute-start(f32[1,16,256]{2,1,0:T(8,128)S(1)} %get-tuple-element.36), channel_id=1, source_target_pairs={{0,1},{1,2},{2,3},{3,4},{4,5},{5,6},{6,7},{7,8},{8,9},{9,10},{10,1... | collective-permute-start | bytes 49160 | tf_op jit(solution)/shard_map/ppermute | solution.py:36
  289.8 5.0 %collective-permute-start.25 = (f32[1,16,256]{2,1,0:T(8,128)S(1)}, f32[1,16,256]{2,1,0:T(8,128)S(1)}, u32[]{:S(2)}, u32[]{:S(2)}) collective-permute-start(f32[1,16,256]{2,1,0:T(8,128)S(1)} %get-tuple-element.31), channel_id=1, source_target_pairs={{1,0},{2,1},{3,2},{4,3},{5,4},{6,5},{7,6},{8,7},{9,8},{10,9},{11,1... | collective-permute-start | bytes 49160 | tf_op jit(solution)/shard_map/ppermute | solution.py:37
  291.7 6.0 %collective-permute-start.26 = (f32[1,16,256]{2,1,0:T(8,128)S(1)}, f32[1,16,256]{2,1,0:T(8,128)S(1)}, u32[]{:S(2)}, u32[]{:S(2)}) collective-permute-start(f32[1,16,256]{2,1,0:T(8,128)S(1)} %get-tuple-element.32), channel_id=1, source_target_pairs={{0,1},{1,2},{2,3},{3,4},{4,5},{5,6},{6,7},{7,8},{8,9},{9,10},{10,1... | collective-permute-start | bytes 49160 | tf_op jit(solution)/shard_map/ppermute | solution.py:36
  298.6 4.3 %collective-permute-start.27 = (f32[1,16,256]{2,1,0:T(8,128)S(1)}, f32[1,16,256]{2,1,0:T(8,128)S(1)}, u32[]{:S(2)}, u32[]{:S(2)}) collective-permute-start(f32[1,16,256]{2,1,0:T(8,128)S(1)} %get-tuple-element.29), channel_id=1, source_target_pairs={{1,0},{2,1},{3,2},{4,3},{5,4},{6,5},{7,6},{8,7},{9,8},{10,9},{11,1... | collective-permute-start | bytes 49160 | tf_op jit(solution)/shard_map/ppermute | solution.py:37
  300.6 6.0 %collective-permute-start.28 = (f32[1,16,256]{2,1,0:T(8,128)S(1)}, f32[1,16,256]{2,1,0:T(8,128)S(1)}, u32[]{:S(2)}, u32[]{:S(2)}) collective-permute-start(f32[1,16,256]{2,1,0:T(8,128)S(1)} %get-tuple-element.30), channel_id=1, source_target_pairs={{0,1},{1,2},{2,3},{3,4},{4,5},{5,6},{6,7},{7,8},{8,9},{9,10},{10,1... | collective-permute-start | bytes 49160 | tf_op jit(solution)/shard_map/ppermute | solution.py:36
  308.1 4.8 %collective-permute-start.29 = (f32[1,16,256]{2,1,0:T(8,128)S(1)}, f32[1,16,256]{2,1,0:T(8,128)S(1)}, u32[]{:S(2)}, u32[]{:S(2)}) collective-permute-start(f32[1,16,256]{2,1,0:T(8,128)S(1)} %get-tuple-element.25), channel_id=1, source_target_pairs={{1,0},{2,1},{3,2},{4,3},{5,4},{6,5},{7,6},{8,7},{9,8},{10,9},{11,1... | collective-permute-start | bytes 49160 | tf_op jit(solution)/shard_map/ppermute | solution.py:37
  310.0 6.0 %collective-permute-start.30 = (f32[1,16,256]{2,1,0:T(8,128)S(1)}, f32[1,16,256]{2,1,0:T(8,128)S(1)}, u32[]{:S(2)}, u32[]{:S(2)}) collective-permute-start(f32[1,16,256]{2,1,0:T(8,128)S(1)} %get-tuple-element.26), channel_id=1, source_target_pairs={{0,1},{1,2},{2,3},{3,4},{4,5},{5,6},{6,7},{7,8},{8,9},{9,10},{10,1... | collective-permute-start | bytes 49160 | tf_op jit(solution)/shard_map/ppermute | solution.py:36
  (7 other events, 18.0 us)
